TPU v7x, 32 devices: a whole 2x2x4 slice. The times are simulated.
32 devices in a mesh: chan: 16 (over z, y, x), cyl: 2 (over core).
Axes of the slice: x: 2, y: 2, z: 4, core: 2. Of those that a mesh axis runs over, the one named last changes fastest.
Arguments:
- volts: bfloat16 [1024, 4, 2, 64, 512], P('chan', 'cyl'), may hold values from -6 to 6
- gain_exponents: int32 [1024, 4], P('chan', 'cyl'), may hold values from -1 to 1
Outputs:
- intensity: float32 [4, 256, 2, 16384], P('cyl', 'chan')
All inputs are finite; a program needn't handle non-finite values.
Results may differ from a plain program's by a relative error of at most 0.0042.
Values may be sent and summed in bfloat16 or wider, within the bound.
A program may use at most 256 MiB of HBM per device.

v0:
```python
import functools
import math

import jax
import jax.numpy as jnp
import ml_dtypes
import numpy as np
from jax import lax
from jax.experimental import pallas as pl
from jax.experimental.pallas import tpu as pltpu
from jax.sharding import PartitionSpec as P

UP = 16
FRAMES = 2


def ns_rows(feeds):
    index = np.arange(feeds)
    theta = (index[None, :] * (index[:, None] - feeds // 2) % feeds) * (2.0 * math.pi / feeds)
    cosine = np.cos(theta) / math.sqrt(feeds)
    sine = np.sin(theta) / math.sqrt(feeds)
    table = np.concatenate(
        [np.concatenate([cosine, sine], axis=1), np.concatenate([-sine, cosine], axis=1)], axis=0
    )
    return table.astype(ml_dtypes.bfloat16)


def fine_rows(cyls, n_cyl, up):
    index = np.arange(up)
    theta = (index[:, None] * index[None, :] % up) * (2.0 * math.pi / up)
    rounded = lambda x: (x / math.sqrt(up)).astype(ml_dtypes.bfloat16).astype(np.float64)
    fine = rounded(np.cos(theta)) - 1j * rounded(np.sin(theta))
    cyl = np.arange(cyls)
    phase = 2.0 * math.pi * cyl[None, :] * (cyl[:, None] - (cyls - 1) / 2.0) / cyls
    weight = np.exp(-1j * phase) / 2.0
    both = np.einsum("ec,km->emck", weight, fine)
    parts = np.stack(
        [np.stack([both.real, -both.imag], axis=3), np.stack([both.imag, both.real], axis=3)], axis=0
    )
    per = cyls // n_cyl
    tables = []
    for rank in range(n_cyl):
        order = [((rank - d) % n_cyl) * per + c for d in range(n_cyl) for c in range(per)]
        tables.append(parts[:, :, :, order].reshape(2 * cyls * up, cyls * 2 * up))
    return np.stack(tables).astype(ml_dtypes.bfloat16)


def beam_kernel(
    cyls, n_cyl, volts_ref, fine_ref, ns_ref, gain_ref, out_ref,
    mid_ref, held_ref, own_sem, send_sem, recv_sem,
):
    step = pl.program_id(0)
    steps = pl.num_programs(0)
    _, _, group, per, pols, times, inputs = held_ref.shape
    feeds = inputs // 2
    blocks = times // UP
    sums = blocks // FRAMES
    rank = lax.axis_index("cyl")

    def own_copy(g):
        rows = pl.ds((rank * steps + g) * group, group)
        return pltpu.make_async_copy(volts_ref.at[rows], held_ref.at[0, g], own_sem.at[g])

    def far_copy(d, g):
        to = lax.rem(rank + d, n_cyl)
        rows = pl.ds((to * steps + g) * group, group)
        return pltpu.make_async_remote_copy(
            src_ref=volts_ref.at[rows],
            dst_ref=held_ref.at[d, g],
            send_sem=send_sem.at[d, g],
            recv_sem=recv_sem.at[d, g],
            device_id={"cyl": to},
            device_id_type=pl.DeviceIdType.MESH,
        )

    @pl.when(step == 0)
    def _():
        own_copy(0).start()
        barrier = pltpu.get_barrier_semaphore()
        for d in range(1, n_cyl):
            pl.semaphore_signal(
                barrier, inc=1, device_id={"cyl": lax.rem(rank + d, n_cyl)},
                device_id_type=pl.DeviceIdType.MESH,
            )
        pl.semaphore_wait(barrier, n_cyl - 1)

        def start(g, carry):
            for d in range(1, n_cyl):
                far_copy(d, g).start()

            @pl.when(g > 0)
            def _():
                own_copy(g).start()

            return carry

        lax.fori_loop(0, steps, start, 0)

    own_copy(step).wait()
    for d in range(1, n_cyl):
        far_copy(d, step).wait()
    volt_refs = [held_ref.at[d, step] for d in range(n_cyl)]
    fine = fine_ref[rank]

    def one_chan(ch, carry):
        for p in range(pols):
            for j in range(blocks):
                rows = jnp.concatenate(
                    [
                        ref[ch, c, p, j * UP : (j + 1) * UP, r * feeds : (r + 1) * feeds]
                        for ref in volt_refs
                        for c in range(per)
                        for r in range(2)
                    ],
                    axis=0,
                )
                got = jnp.dot(fine, rows, preferred_element_type=jnp.float32).astype(jnp.bfloat16)
                for s in range(2):
                    for e in range(cyls):
                        at = (s * cyls + e) * UP
                        mid_ref[p * blocks + j, e, ch, :, s * feeds : (s + 1) * feeds] = got[at : at + UP]
        return carry

    lax.fori_loop(0, group, one_chan, 0)
    wide = group * UP
    pair = 2 if cyls % 2 == 0 else 1
    ns = ns_ref[...]
    for q in range(FRAMES):
        for e in range(0, cyls, pair):
            total = None
            for p in range(pols):
                for j in range(q * sums, (q + 1) * sums):
                    block = mid_ref[p * blocks + j, e : e + pair].reshape(pair * wide, inputs)
                    spectra = lax.dot_general(
                        ns, block, (((1,), (1,)), ((), ())), preferred_element_type=jnp.float32
                    )
                    squared = spectra * spectra
                    power = squared[:feeds] + squared[feeds:]
                    total = power if total is None else total + power
            for i in range(pair):
                scaled = total[:, i * wide : (i + 1) * wide] * gain_ref[0, e + i : e + i + 1, :]
                out_ref[0, e + i, q] = scaled.astype(jnp.bfloat16)


def spread_kernel(in_ref, out_ref):
    sources, _, frames, steps, near, wide = in_ref.shape

    def one(source, carry):
        at = pl.multiple_of(source * (steps * wide), 128)
        for g in range(steps):
            rows = [in_ref[source, 0, q, g].astype(jnp.float32) for q in range(frames)]
            out_ref[0, :, :, pl.ds(at + g * wide, wide)] = jnp.stack(rows, axis=1)
        return carry

    lax.fori_loop(0, sources, one, 0)


def spread(power):
    sources, per, frames, steps, near, wide = power.shape
    lanes = sources * steps * wide
    return pl.pallas_call(
        spread_kernel,
        out_shape=jax.ShapeDtypeStruct((per, near, frames, lanes), jnp.float32),
        grid=(per,),
        in_specs=[pl.BlockSpec((sources, 1, frames, steps, near, wide), lambda e: (0, e, 0, 0, 0, 0))],
        out_specs=pl.BlockSpec((1, near, frames, lanes), lambda e: (e, 0, 0, 0)),
        compiler_params=pltpu.CompilerParams(dimension_semantics=("arbitrary",)),
        name="spread",
    )(power)


def local(n_chan, n_cyl, volts, gain_exponents):
    chans, per, pols, times, inputs = volts.shape
    feeds = inputs // 2
    cyls = per * n_cyl
    own = chans // n_cyl
    group = math.gcd(8, own)
    steps = own // group
    wide = group * UP
    blocks = times // UP
    rank = lax.axis_index("cyl")
    gains = [lax.dynamic_slice_in_dim(gain_exponents, rank * own, own, 0)]
    for d in range(1, n_cyl):
        ring = [(k, (k + d) % n_cyl) for k in range(n_cyl)]
        to = (rank + d) % n_cyl
        gains.append(
            lax.ppermute(lax.dynamic_slice_in_dim(gain_exponents, to * own, own, 0), "cyl", ring)
        )
    stacked = jnp.stack(gains)
    order = (rank - jnp.arange(n_cyl, dtype=jnp.int32)) % n_cyl
    exps = jnp.take(stacked, order, axis=0)
    exps = jnp.transpose(exps, (0, 2, 1)).reshape(cyls, steps, group)
    scale = jnp.exp2(2.0 * exps.astype(jnp.float32)) / (pols * (blocks // FRAMES))
    scale = jnp.transpose(jnp.repeat(scale, UP, axis=2), (1, 0, 2))

    fine = jnp.asarray(fine_rows(cyls, n_cyl, UP))
    ns = jnp.asarray(ns_rows(feeds))
    power = pl.pallas_call(
        functools.partial(beam_kernel, cyls, n_cyl),
        out_shape=jax.ShapeDtypeStruct((steps, cyls, FRAMES, feeds, wide), jnp.bfloat16),
        grid=(steps,),
        in_specs=[
            pl.BlockSpec(memory_space=pl.ANY),
            pl.BlockSpec(fine.shape, lambda g: (0, 0, 0)),
            pl.BlockSpec(ns.shape, lambda g: (0, 0)),
            pl.BlockSpec((1, cyls, wide), lambda g: (g, 0, 0)),
        ],
        out_specs=pl.BlockSpec((1, cyls, FRAMES, feeds, wide), lambda g: (g, 0, 0, 0, 0)),
        scratch_shapes=[
            pltpu.VMEM((pols * blocks, cyls, group, UP, inputs), jnp.bfloat16),
            pltpu.VMEM((n_cyl, steps, group, per, pols, times, inputs), jnp.bfloat16),
            pltpu.SemaphoreType.DMA((steps,)),
            pltpu.SemaphoreType.DMA((n_cyl, steps)),
            pltpu.SemaphoreType.DMA((n_cyl, steps)),
        ],
        compiler_params=pltpu.CompilerParams(
            dimension_semantics=("arbitrary",), collective_id=0, has_side_effects=True
        ),
        name="beams",
    )(volts, fine, ns, scale)

    near = feeds // n_chan
    power = power.reshape(steps, n_cyl, per, FRAMES, n_chan, near, wide)
    power = jnp.transpose(power, (4, 1, 2, 3, 0, 5, 6))
    power = power.reshape(n_chan * n_cyl, per, FRAMES, steps, near, wide)
    power = lax.all_to_all(power, ("chan", "cyl"), split_axis=0, concat_axis=0, tiled=True)
    if (steps * wide) % 128 == 0:
        return spread(power)
    power = jnp.transpose(power, (1, 4, 2, 0, 3, 5))
    return power.reshape(per, near, FRAMES, -1).astype(jnp.float32)


def solution(mesh):
    return jax.shard_map(
        functools.partial(local, mesh.shape["chan"], mesh.shape["cyl"]),
        mesh=mesh,
        in_specs=(P("chan", "cyl", None, None, None), P("chan", "cyl")),
        out_specs=P("cyl", "chan", None, None),
        check_vma=False,
    )
```

profile of v0, /device:TPU:0, one launch (start us, length us, event | category | flops | bytes accessed | tf_op | source)
XLA Modules:
  0.0 94.0 jit_solution(18127062370597439523)
XLA Ops:
  0.0 0.8 dynamic-slice_bitcast_fusion
  0.8 0.5 collective-permute-start
  1.4 0.8 collective-permute-done
  2.1 0.6 gather_fusion
  2.7 0.1 multiply_bitcast_fusion
  2.8 0.1 div.10
  2.9 0.1 broadcast_in_dim.15
  3.0 0.7 reshape.70
  3.7 25.4 %beams.1 = bf16[4,4,2,256,128]{4,3,2,1,0:T(8,128)(2,1)} custom-call(bf16[64,2,2,64,512]{4,3,2,1,0:T(8,128)(2,1)} %volts_ref.1, bf16[2,128,128]{2,1,0:T(8,128)(2,1)} %constant.57.clone.fine_ref, bf16[512,512]{1,0:T(8,128)(2,1)} %constant.58.clone.ns_ref, f32[4,4,128]{2,1,0:T(4,128)} %bitcast.18), custom_call_target="tpu_custom_call" | custom-call | tf_op jit(solution)/shard_map/beams/pallas_call | solution.py:198
  29.1 2.2 %copy.6 = bf16[4,2,2,2,16,16,128]{6,5,0,3,2,1,4:T(8,128)(2,1)S(1)} copy(bf16[4,2,2,2,16,16,128]{6,5,4,3,2,1,0:T(8,128)(2,1)} %bitcast.16) | data formatting | bytes 4194304 | tf_op jit(solution)/shard_map/reshape | solution.py:223
  31.3 55.8 %all_to_all.5.in_ref = bf16[32,2,2,4,16,128]{5,4,3,2,1,0:T(8,128)(2,1)} all-to-all(bf16[32,2,2,4,16,128]{5,4,3,2,1,0:T(8,128)(2,1)S(1)} %bitcast.17), channel_id=1, replica_groups=mesh['chan'=16,'cyl'=2] {'chan','cyl'}, dimensions={0} | all-to-all | bytes 4194304 | tf_op jit(solution)/shard_map/all_to_all | solution.py:226
  87.1 6.9 %spread.1 = f32[2,16,2,16384]{3,2,1,0:T(2,128)} custom-call(bf16[32,2,2,4,16,128]{5,4,3,2,1,0:T(8,128)(2,1)} %all_to_all.5.in_ref), custom_call_target="tpu_custom_call" | custom-call | tf_op jit(solution)/shard_map/spread/pallas_call | solution.py:161
  (5 shorter events, 0.0 us)
Async XLA Ops:
  0.8 1.3 %collective-permute-start = (s32[32,2]{0,1:T(2,128)S(1)}, s32[32,2]{0,1:T(2,128)S(1)}, u32[]{:S(2)}, u32[]{:S(2)}) collective-permute-start(s32[32,2]{0,1:T(2,128)S(1)} %get-tuple-element.6), channel_id=1, source_target_pairs={{0,1},{1,0},{2,3},{3,2},{4,5},{5,4},{6,7},{7,6},{8,9},{9,8},{10,11... | collective-permute-start | bytes 776 | tf_op jit(solution)/shard_map/ppermute | solution.py:187
where the time goes:
time: 94.2 us; the launch traced here: 94 us
  blocking collectives  55.8 us (59%)
  Pallas kernels  32.3 us (34%)
  local copies, waits for them, and re-layouts  4.47 us (5%)
    all_to_all x1, blocking collectives, local(): lax.all_to_all(power, ('chan', 'cyl'), split_axis=0, concat_axis=0, tiled...  55.8 us
    pallas_call x1, Pallas kernels, local(): pl.pallas_call(functools.partial(beam_kernel, cyls, n_cyl), out_shape=jax...  25.4 us
    pallas_call x1, Pallas kernels, spread(): pl.pallas_call(spread_kernel, out_shape=jax.ShapeDtypeStruct((per, near,...  6.87 us
    reshape x1, local copies, waits for them, and re-layouts, local(): power = power.reshape(steps, n_cyl, per, FRAMES, n_chan, near, wide)  2.2 us
  transfers between devices with their start and end apart: 1, of which 1 were waited for; matrix products, arithmetic and copies ran while one was open for 0% of the time, Pallas kernels for 0%

commit v1 on v0

--- a/solution.py
+++ b/solution.py
@@ -167,6 +167,286 @@
         compiler_params=pltpu.CompilerParams(dimension_semantics=("arbitrary",)),
         name="spread",
     )(power)
+
+
+def half_rows(feeds):
+    half = feeds // 2
+    table = np.asarray(ns_rows(feeds)).reshape(2, half, 2, 2, feeds)[..., :half]
+    return np.transpose(table, (2, 0, 1, 3, 4)).reshape(2, feeds, feeds)
+
+
+def fused_kernel(
+    n_chan, n_cyl, volts_ref, gains_ref, fine_hbm, ns_hbm, out_ref,
+    held_ref, mid_ref, send_ref, recv_ref, exps_ref, scale_ref, fine_ref, ns_ref,
+    own_sem, volt_send_sem, volt_recv_sem, exp_sem, exp_send_sem, exp_recv_sem, table_sem,
+    send_sem, recv_sem,
+):
+    chip = lax.axis_index("chan")
+    rank = lax.axis_index("cyl")
+    me = chip * n_cyl + rank
+    devices = n_chan * n_cyl
+    _, stages, group, per, pols, times, inputs = held_ref.shape
+    pieces = volt_recv_sem.shape[2]
+    piece = group // pieces
+    blocks = times // UP
+    feeds = inputs // 2
+    half = feeds // 2
+    cyls = per * n_cyl
+    steps = stages // FRAMES
+    own = steps * group
+    wide = group * UP
+    near = feeds // n_chan
+
+    def volt_rows(to, s, first, count):
+        at = to * own + (s // FRAMES) * group + first
+        time = pl.multiple_of((s % FRAMES) * times, times)
+        return volts_ref.at[pl.ds(at, count), :, :, pl.ds(time, times), :]
+
+    def own_copy(s):
+        return pltpu.make_async_copy(volt_rows(rank, s, 0, group), held_ref.at[rank, s], own_sem.at[s])
+
+    def far_copy(d, s, i):
+        to = lax.rem(rank + d, n_cyl)
+        return pltpu.make_async_remote_copy(
+            src_ref=volt_rows(to, s, i * piece, piece),
+            dst_ref=held_ref.at[rank, s, pl.ds(i * piece, piece)],
+            send_sem=volt_send_sem.at[d],
+            recv_sem=volt_recv_sem.at[d, s, i],
+            device_id={"cyl": to},
+            device_id_type=pl.DeviceIdType.MESH,
+        )
+
+    def far_arrived(d, s, i):
+        source = lax.rem(rank + n_cyl - d, n_cyl)
+        there = held_ref.at[source, s, pl.ds(i * piece, piece)]
+        return pltpu.make_async_copy(there, there, volt_recv_sem.at[d, s, i])
+
+    def exp_copy(d):
+        return pltpu.make_async_remote_copy(
+            src_ref=gains_ref,
+            dst_ref=exps_ref.at[rank],
+            send_sem=exp_send_sem.at[d],
+            recv_sem=exp_recv_sem.at[d],
+            device_id={"cyl": lax.rem(rank + d, n_cyl)},
+            device_id_type=pl.DeviceIdType.MESH,
+        )
+
+    fine_copy = pltpu.make_async_copy(fine_hbm, fine_ref, table_sem.at[0])
+    ns_copy = pltpu.make_async_copy(ns_hbm, ns_ref, table_sem.at[1])
+    own_exps = pltpu.make_async_copy(gains_ref, exps_ref.at[rank], exp_sem)
+
+    barrier = pltpu.get_barrier_semaphore()
+
+    def greet(i, carry):
+        to = lax.rem(me + i, devices)
+        pl.semaphore_signal(
+            barrier, inc=1, device_id={"chan": to // n_cyl, "cyl": lax.rem(to, n_cyl)},
+            device_id_type=pl.DeviceIdType.MESH,
+        )
+        return carry
+
+    lax.fori_loop(1, devices, greet, 0)
+    fine_copy.start()
+    own_exps.start()
+    own_copy(0).start()
+    ns_copy.start()
+
+    def start_own(s, carry):
+        own_copy(s).start()
+        return carry
+
+    lax.fori_loop(1, stages, start_own, 0)
+    pl.semaphore_wait(barrier, devices - 1)
+    for d in range(1, n_cyl):
+        exp_copy(d).start()
+
+    def start_far(n, carry):
+        for d in range(1, n_cyl):
+            far_copy(d, n // pieces, n % pieces).start()
+        return carry
+
+    lax.fori_loop(0, stages * pieces, start_far, 0)
+    fine_copy.wait()
+    own_exps.wait()
+    ns_copy.wait()
+    for d in range(1, n_cyl):
+        exp_copy(d).wait()
+    chans = exps_ref.shape[2]
+    lane = lax.broadcasted_iota(jnp.int32, (chans, own * UP), 1) // UP + rank * own
+    pick = (lane == lax.broadcasted_iota(jnp.int32, (chans, own * UP), 0)).astype(jnp.float32)
+    exps = jnp.concatenate([exps_ref[i] for i in range(n_cyl)], axis=0).astype(jnp.float32)
+    spread_exps = jnp.dot(exps, pick, preferred_element_type=jnp.float32)
+    scale = jnp.exp2(2.0 * spread_exps) / (pols * blocks)
+    for g in range(steps):
+        scale_ref[g] = scale[:, g * wide : (g + 1) * wide]
+
+    def one_stage(s, carry):
+        own_copy(s).wait()
+        fine = fine_ref[...]
+
+        def one_piece(i, inner):
+            for d in range(1, n_cyl):
+                far_arrived(d, s, i).wait()
+            for c0 in range(piece):
+                ch = i * piece + c0
+                for p in range(pols):
+                    for j in range(blocks):
+                        rows = jnp.concatenate(
+                            [
+                                held_ref[o, s, ch, c, p, j * UP : (j + 1) * UP, r * feeds : (r + 1) * feeds]
+                                for o in range(n_cyl)
+                                for c in range(per)
+                                for r in range(2)
+                            ],
+                            axis=0,
+                        )
+                        got = jnp.dot(fine, rows, preferred_element_type=jnp.float32)
+                        low, high = got[:, :half], got[:, half:]
+                        both = ((low + high).astype(jnp.bfloat16), (low - high).astype(jnp.bfloat16))
+                        for odd in range(2):
+                            for r in range(2):
+                                for e in range(cyls):
+                                    at = (r * cyls + e) * UP
+                                    mid_ref[p * blocks + j, odd, e, ch, :, r * half : (r + 1) * half] = (
+                                        both[odd][at : at + UP]
+                                    )
+            return inner
+
+        lax.fori_loop(0, pieces, one_piece, 0)
+        for owner in range(n_cyl):
+            parts = []
+            for odd in range(2):
+                ns = ns_ref[odd]
+                total = None
+                for b in range(pols * blocks):
+                    block = mid_ref[b, odd, owner * per : (owner + 1) * per].reshape(per * wide, feeds)
+                    spectra = lax.dot_general(
+                        ns, block, (((1,), (1,)), ((), ())), preferred_element_type=jnp.float32
+                    )
+                    squared = spectra * spectra
+                    power = squared[:half] + squared[half:]
+                    total = power if total is None else total + power
+                parts.append(total)
+            for e in range(per):
+                factor = scale_ref[s // FRAMES, owner * per + e : owner * per + e + 1, :]
+                scaled = [
+                    (part[:, e * wide : (e + 1) * wide] * factor).reshape(n_chan, near // 2, wide)
+                    for part in parts
+                ]
+                send_ref[s, owner, :, e] = jnp.concatenate(scaled, axis=1).astype(jnp.bfloat16)
+
+            def send(i, inner):
+                to = lax.rem(chip + n_chan // 2 + i, n_chan)
+                here = jnp.logical_and(to == chip, rank == owner)
+
+                @pl.when(here)
+                def _():
+                    pltpu.make_async_copy(
+                        send_ref.at[s, owner, to], recv_ref.at[s, me], recv_sem.at[s]
+                    ).start()
+
+                @pl.when(jnp.logical_not(here))
+                def _():
+                    pltpu.make_async_remote_copy(
+                        src_ref=send_ref.at[s, owner, to],
+                        dst_ref=recv_ref.at[s, me],
+                        send_sem=send_sem,
+                        recv_sem=recv_sem.at[s],
+                        device_id={"chan": to, "cyl": owner},
+                        device_id_type=pl.DeviceIdType.MESH,
+                    ).start()
+
+                return inner
+
+            lax.fori_loop(0, n_chan, send, 0)
+        return carry
+
+    lax.fori_loop(0, stages, one_stage, 0)
+
+    depth = devices * stages
+
+    def spread_stage(s, carry):
+        pltpu.make_async_copy(recv_ref.at[s], recv_ref.at[s], recv_sem.at[s]).wait()
+
+        def one(source, inner):
+            row = (source * steps + s // FRAMES) * FRAMES + s % FRAMES
+            for e in range(per):
+                tile = recv_ref[s, source, e].astype(jnp.float32)
+                for odd in range(2):
+                    at = (e * near + odd) * depth + row
+                    out_ref[pl.ds(at, near // 2, 2 * depth), :] = tile[odd * (near // 2) : (odd + 1) * (near // 2)]
+            return inner
+
+        lax.fori_loop(0, devices, one, 0)
+        return carry
+
+    lax.fori_loop(0, stages, spread_stage, 0)
+    sent = recv_ref.at[:, : devices - 1]
+    pltpu.make_async_copy(sent, sent, send_sem).wait()
+    for d in range(1, n_cyl):
+        pltpu.make_async_copy(held_ref.at[0], held_ref.at[0], volt_send_sem.at[d]).wait()
+
+
+def fused(n_chan, n_cyl, volts, gain_exponents):
+    chans, per, pols, times, inputs = volts.shape
+    feeds = inputs // 2
+    cyls = per * n_cyl
+    own = chans // n_cyl
+    group = 128 // UP
+    steps = own // group
+    stages = steps * FRAMES
+    span = times // FRAMES
+    blocks = span // UP
+    near = feeds // n_chan
+    devices = n_chan * n_cyl
+    wide = group * UP
+    pieces = 4
+    fine = jnp.asarray(fine_rows(cyls, 1, UP)[0])
+    ns = jnp.asarray(half_rows(feeds))
+    dma = pltpu.SemaphoreType.DMA
+    out = pl.pallas_call(
+        functools.partial(fused_kernel, n_chan, n_cyl),
+        out_shape=jax.ShapeDtypeStruct((per * near * devices * stages, wide), jnp.float32),
+        in_specs=[pl.BlockSpec(memory_space=pl.ANY)] * 4,
+        out_specs=pl.BlockSpec(memory_space=pltpu.VMEM),
+        scratch_shapes=[
+            pltpu.VMEM((n_cyl, stages, group, per, pols, span, inputs), jnp.bfloat16),
+            pltpu.VMEM((pols * blocks, 2, cyls, group, UP, feeds), jnp.bfloat16),
+            pltpu.VMEM((stages, n_cyl, n_chan, per, near, wide), jnp.bfloat16),
+            pltpu.VMEM((stages, devices, per, near, wide), jnp.bfloat16),
+            pltpu.VMEM((n_cyl, per, chans), jnp.int32),
+            pltpu.VMEM((steps, cyls, wide), jnp.float32),
+            pltpu.VMEM(fine.shape, jnp.bfloat16),
+            pltpu.VMEM(ns.shape, jnp.bfloat16),
+            dma((stages,)),
+            dma((n_cyl,)),
+            dma((n_cyl, stages, pieces)),
+            dma,
+            dma((n_cyl,)),
+            dma((n_cyl,)),
+            dma((2,)),
+            dma,
+            dma((stages,)),
+        ],
+        compiler_params=pltpu.CompilerParams(
+            collective_id=0, has_side_effects=True, vmem_limit_bytes=48 * 1024 * 1024
+        ),
+        name="fused",
+    )(volts, gain_exponents.T, fine, ns)
+    out = out.reshape(per, near, devices * steps, FRAMES, wide)
+    return jnp.transpose(out, (0, 1, 3, 2, 4)).reshape(per, near, FRAMES, -1)
+
+
+def fits(n_chan, n_cyl, volts):
+    chans, per, pols, times, inputs = volts.shape
+    own = chans // n_cyl
+    feeds = inputs // 2
+    return (
+        own % (128 // UP) == 0
+        and feeds % (16 * n_chan) == 0
+        and feeds % 256 == 0
+        and times % (FRAMES * UP) == 0
+    )
 
 
 def local(n_chan, n_cyl, volts, gain_exponents):
@@ -230,9 +510,15 @@
     return power.reshape(per, near, FRAMES, -1).astype(jnp.float32)
 
 
+def either(n_chan, n_cyl, volts, gain_exponents):
+    if fits(n_chan, n_cyl, volts):
+        return fused(n_chan, n_cyl, volts, gain_exponents)
+    return local(n_chan, n_cyl, volts, gain_exponents)
+
+
 def solution(mesh):
     return jax.shard_map(
-        functools.partial(local, mesh.shape["chan"], mesh.shape["cyl"]),
+        functools.partial(either, mesh.shape["chan"], mesh.shape["cyl"]),
         mesh=mesh,
         in_specs=(P("chan", "cyl", None, None, None), P("chan", "cyl")),
         out_specs=P("cyl", "chan", None, None),

time: 94.2 us -> 62.5 us (0.66)
  blocking collectives: 55.8 us -> 0 us
  Pallas kernels: 32.3 us -> 57.4 us
    all_to_all x1 -> x0, blocking collectives: 55.8 us -> none  [local(): lax.all_to_all(power, ('chan', 'cyl'), split_axis=0, concat_axis=0, tiled...]
    pallas_call x2 -> x1, Pallas kernels: 32.3 us -> 57.4 us  [fused(): pl.pallas_call(functools.partial(fused_kernel, n_chan, n_cyl), out_shape=...]
    unnamed x0 -> x7, local copies, waits for them, and re-layouts: none -> 4.4 us
    reshape x2 -> x0, local copies, waits for them, and re-layouts: 2.9 us -> none  [the longest x1 2.2 us: local(): power = power.reshape(steps, n_cyl, per, FRAMES, n_chan, near, wide)]
  transfers between devices with their start and end apart: 1 -> 0, of which waited for: 1 -> 0; matrix products, arithmetic and copies ran while one was open for 0% -> 0% of each run, Pallas kernels for 0% -> 0%
where the time goes in v1:
time: 62.5 us; the launch traced here: 61.8 us
  Pallas kernels  57.4 us (92%)
  local copies, waits for them, and re-layouts  4.4 us (7%)
    pallas_call x1, Pallas kernels, fused(): pl.pallas_call(functools.partial(fused_kernel, n_chan, n_cyl), out_shape=...  57.4 us
    unnamed x7, local copies, waits for them, and re-layouts  4.4 us

profile of v1, /device:TPU:0, one launch (start us, length us, event | category | flops | bytes accessed | tf_op | source)
XLA Modules:
  0.0 61.8 jit_solution(12566917873569453909)
XLA Ops:
  0.0 0.0 copy-start
  0.0 0.9 %copy-done = bf16[2,256,256]{2,1,0:T(8,128)(2,1)S(1)} copy-done((bf16[2,256,256]{2,1,0:T(8,128)(2,1)S(1)}, bf16[2,256,256]{2,1,0:T(8,128)(2,1)}, u32[]{:S(2)}) %copy-start) | copy-done | bytes 262168
  1.0 0.0 copy-start.1
  1.0 0.8 %copy-done.1 = bf16[128,128]{1,0:T(8,128)(2,1)S(1)} copy-done((bf16[128,128]{1,0:T(8,128)(2,1)S(1)}, bf16[128,128]{1,0:T(8,128)(2,1)}, u32[]{:S(2)}) %copy-start.1) | copy-done | bytes 32792
  1.7 0.0 copy-start.2
  1.7 0.7 %copy-done.2 = s32[64,2]{0,1:T(2,128)S(1)} copy-done((s32[64,2]{0,1:T(2,128)S(1)}, s32[64,2]{0,1:T(2,128)}, u32[]{:S(2)}) %copy-start.2) | copy-done | bytes 536
  2.4 57.4 %fused.1 = f32[8192,128]{1,0:T(8,128)S(1)} custom-call(bf16[64,2,2,64,512]{4,3,2,1,0:T(8,128)(2,1)} %volts_ref.1, s32[2,64]{1,0:T(2,128)S(1)} %bitcast.7, bf16[128,128]{1,0:T(8,128)(2,1)S(1)} %copy-done.1, bf16[2,256,256]{2,1,0:T(8,128)(2,1)S(1)} %copy-done), custom_call_target="tpu_custom_call" | custom-call | tf_op jit(solution)/shard_map/fused/pallas_call | solution.py:407
  59.8 2.0 %copy.7 = f32[2,16,2,16384]{3,2,1,0:T(2,128)} copy(f32[2,16,2,16384]{3,2,1,0:T(2,128)S(1)} %bitcast.6) | data formatting | bytes 8388608
Async XLA Ops:
  0.0 0.9 %copy-start = (bf16[2,256,256]{2,1,0:T(8,128)(2,1)S(1)}, bf16[2,256,256]{2,1,0:T(8,128)(2,1)}, u32[]{:S(2)}) copy-start(bf16[2,256,256]{2,1,0:T(8,128)(2,1)} %constant.5.clone.ns_hbm) | copy-start | bytes 786436
  1.0 0.8 %copy-start.1 = (bf16[128,128]{1,0:T(8,128)(2,1)S(1)}, bf16[128,128]{1,0:T(8,128)(2,1)}, u32[]{:S(2)}) copy-start(bf16[128,128]{1,0:T(8,128)(2,1)} %constant.4.clone.fine_hbm) | copy-start | bytes 98308
  1.7 0.7 %copy-start.2 = (s32[64,2]{0,1:T(2,128)S(1)}, s32[64,2]{0,1:T(2,128)}, u32[]{:S(2)}) copy-start(s32[64,2]{0,1:T(2,128)} %param.5) | copy-start | bytes 1540

commit v2 on v1

--- a/solution.py
+++ b/solution.py
@@ -179,7 +179,7 @@
     n_chan, n_cyl, volts_ref, gains_ref, fine_hbm, ns_hbm, out_ref,
     held_ref, mid_ref, send_ref, recv_ref, exps_ref, scale_ref, fine_ref, ns_ref,
     own_sem, volt_send_sem, volt_recv_sem, exp_sem, exp_send_sem, exp_recv_sem, table_sem,
-    send_sem, recv_sem,
+    send_sem, recv_sem, pair_sem, go_sem,
 ):
     chip = lax.axis_index("chan")
     rank = lax.axis_index("cyl")
@@ -236,36 +236,57 @@
     own_exps = pltpu.make_async_copy(gains_ref, exps_ref.at[rank], exp_sem)
 
     barrier = pltpu.get_barrier_semaphore()
-
-    def greet(i, carry):
-        to = lax.rem(me + i, devices)
-        pl.semaphore_signal(
-            barrier, inc=1, device_id={"chan": to // n_cyl, "cyl": lax.rem(to, n_cyl)},
-            device_id_type=pl.DeviceIdType.MESH,
-        )
-        return carry
-
-    lax.fori_loop(1, devices, greet, 0)
+    mesh_id = pl.DeviceIdType.MESH
+
+    @pl.when(rank == 0)
+    def _():
+        pl.semaphore_signal(barrier, inc=1, device_id={"cyl": 1}, device_id_type=mesh_id)
+
+    own_copy(0).start()
     fine_copy.start()
     own_exps.start()
-    own_copy(0).start()
     ns_copy.start()
+
+    @pl.when(rank == 1)
+    def _():
+        pl.semaphore_wait(barrier, 1)
+        pl.semaphore_signal(pair_sem, inc=1, device_id={"cyl": 0}, device_id_type=mesh_id)
+
+    @pl.when(rank == 0)
+    def _():
+        pl.semaphore_wait(pair_sem, 1)
+
+        def greet(i, carry):
+            to = lax.rem(chip + i, n_chan)
+            pl.semaphore_signal(barrier, inc=1, device_id={"chan": to}, device_id_type=mesh_id)
+            return carry
+
+        lax.fori_loop(1, n_chan, greet, 0)
+
+    def all_here():
+        @pl.when(rank == 0)
+        def _():
+            pl.semaphore_wait(barrier, n_chan - 1)
+            pl.semaphore_signal(go_sem, inc=1, device_id={"cyl": 1}, device_id_type=mesh_id)
+
+        @pl.when(rank == 1)
+        def _():
+            pl.semaphore_wait(go_sem, 1)
 
     def start_own(s, carry):
         own_copy(s).start()
         return carry
-
-    lax.fori_loop(1, stages, start_own, 0)
-    pl.semaphore_wait(barrier, devices - 1)
-    for d in range(1, n_cyl):
-        exp_copy(d).start()
 
     def start_far(n, carry):
         for d in range(1, n_cyl):
             far_copy(d, n // pieces, n % pieces).start()
         return carry
 
-    lax.fori_loop(0, stages * pieces, start_far, 0)
+    lax.fori_loop(0, pieces, start_far, 0)
+    for d in range(1, n_cyl):
+        exp_copy(d).start()
+    lax.fori_loop(1, stages, start_own, 0)
+    lax.fori_loop(pieces, stages * pieces, start_far, 0)
     fine_copy.wait()
     own_exps.wait()
     ns_copy.wait()
@@ -335,8 +356,12 @@
                 ]
                 send_ref[s, owner, :, e] = jnp.concatenate(scaled, axis=1).astype(jnp.bfloat16)
 
+            if owner == 0:
+                pl.when(s == 0)(all_here)
+
             def send(i, inner):
-                to = lax.rem(chip + n_chan // 2 + i, n_chan)
+                side = lax.rem(chip // (n_chan // 2) + 1 + i // (n_chan // 2), 2)
+                to = side * (n_chan // 2) + lax.rem(chip + 1 + i, n_chan // 2)
                 here = jnp.logical_and(to == chip, rank == owner)
 
                 @pl.when(here)
@@ -403,11 +428,12 @@
     pieces = 4
     fine = jnp.asarray(fine_rows(cyls, 1, UP)[0])
     ns = jnp.asarray(half_rows(feeds))
+    operands = (volts, gain_exponents.T, fine, ns)
     dma = pltpu.SemaphoreType.DMA
     out = pl.pallas_call(
         functools.partial(fused_kernel, n_chan, n_cyl),
         out_shape=jax.ShapeDtypeStruct((per * near * devices * stages, wide), jnp.float32),
-        in_specs=[pl.BlockSpec(memory_space=pl.ANY)] * 4,
+        in_specs=[pl.BlockSpec(memory_space=pltpu.HBM)] * 4,
         out_specs=pl.BlockSpec(memory_space=pltpu.VMEM),
         scratch_shapes=[
             pltpu.VMEM((n_cyl, stages, group, per, pols, span, inputs), jnp.bfloat16),
@@ -427,12 +453,14 @@
             dma((2,)),
             dma,
             dma((stages,)),
+            pltpu.SemaphoreType.REGULAR,
+            pltpu.SemaphoreType.REGULAR,
         ],
         compiler_params=pltpu.CompilerParams(
             collective_id=0, has_side_effects=True, vmem_limit_bytes=48 * 1024 * 1024
         ),
         name="fused",
-    )(volts, gain_exponents.T, fine, ns)
+    )(*[pltpu.with_memory_space_constraint(x, pltpu.HBM) for x in operands])
     out = out.reshape(per, near, devices * steps, FRAMES, wide)
     return jnp.transpose(out, (0, 1, 3, 2, 4)).reshape(per, near, FRAMES, -1)
 
@@ -442,7 +470,9 @@
     own = chans // n_cyl
     feeds = inputs // 2
     return (
-        own % (128 // UP) == 0
+        n_cyl == 2
+        and n_chan % 2 == 0
+        and own % (128 // UP) == 0
         and feeds % (16 * n_chan) == 0
         and feeds % 256 == 0
         and times % (FRAMES * UP) == 0

time: 62.5 us -> 59.7 us (0.955)
  local copies, waits for them, and re-layouts: 4.4 us -> 2.02 us
    unnamed x7 -> x1, local copies, waits for them, and re-layouts: 4.4 us -> 2.02 us
where the time goes in v2:
time: 59.7 us; the launch traced here: 58.9 us
  Pallas kernels  56.8 us (95%)
  local copies, waits for them, and re-layouts  2.02 us (3%)
    pallas_call x1, Pallas kernels, fused(): pl.pallas_call(functools.partial(fused_kernel, n_chan, n_cyl), out_shape=...  56.8 us
    unnamed x1, local copies, waits for them, and re-layouts  2.02 us

profile of v2, /device:TPU:0, one launch (start us, length us, event | category | flops | bytes accessed | tf_op | source)
XLA Modules:
  0.0 58.9 jit_solution(376968880622290792)
XLA Ops:
  0.0 56.8 %fused.1 = f32[8192,128]{1,0:T(8,128)S(1)} custom-call(bf16[64,2,2,64,512]{4,3,2,1,0:T(8,128)(2,1)} %volts_ref.1, s32[2,64]{1,0:T(2,128)} %bitcast.7, bf16[128,128]{1,0:T(8,128)(2,1)} %constant.4.clone.fine_hbm, bf16[2,256,256]{2,1,0:T(8,128)(2,1)} %constant.5.clone.ns_hbm), custom_call_target="tpu_custom_call" | custom-call | tf_op jit(solution)/shard_map/fused/pallas_call | solution.py:433
  56.8 2.0 %copy.7 = f32[2,16,2,16384]{3,2,1,0:T(2,128)} copy(f32[2,16,2,16384]{3,2,1,0:T(2,128)S(1)} %bitcast.6) | data formatting | bytes 8388608

commit v3 on v2

--- a/solution.py
+++ b/solution.py
@@ -177,9 +177,10 @@
 
 def fused_kernel(
     n_chan, n_cyl, volts_ref, gains_ref, fine_hbm, ns_hbm, out_ref,
-    held_ref, mid_ref, send_ref, recv_ref, exps_ref, scale_ref, fine_ref, ns_ref,
+    held_ref, mid_ref, head_out_ref, send_ref, head_in_ref, recv_ref,
+    exps_ref, head_scale_ref, scale_ref, fine_ref, ns_ref,
     own_sem, volt_send_sem, volt_recv_sem, exp_sem, exp_send_sem, exp_recv_sem, table_sem,
-    send_sem, recv_sem, pair_sem, go_sem,
+    head_send_sem, head_recv_sem, send_sem, recv_sem, pair_sem, go_sem,
 ):
     chip = lax.axis_index("chan")
     rank = lax.axis_index("cyl")
@@ -196,6 +197,8 @@
     own = steps * group
     wide = group * UP
     near = feeds // n_chan
+    part = group // per
+    slim = part * UP
 
     def volt_rows(to, s, first, count):
         at = to * own + (s // FRAMES) * group + first
@@ -242,6 +245,16 @@
     def _():
         pl.semaphore_signal(barrier, inc=1, device_id={"cyl": 1}, device_id_type=mesh_id)
 
+    @pl.when(rank == 1)
+    def _():
+        pl.semaphore_signal(barrier, inc=1, device_id={"cyl": 0}, device_id_type=mesh_id)
+
+    def greet(i, carry):
+        to = lax.rem(chip + i, n_chan)
+        pl.semaphore_signal(barrier, inc=1, device_id={"chan": to, "cyl": 0}, device_id_type=mesh_id)
+        return carry
+
+    lax.fori_loop(1, n_chan, greet, 0)
     own_copy(0).start()
     fine_copy.start()
     own_exps.start()
@@ -256,17 +269,10 @@
     def _():
         pl.semaphore_wait(pair_sem, 1)
 
-        def greet(i, carry):
-            to = lax.rem(chip + i, n_chan)
-            pl.semaphore_signal(barrier, inc=1, device_id={"chan": to}, device_id_type=mesh_id)
-            return carry
-
-        lax.fori_loop(1, n_chan, greet, 0)
-
     def all_here():
         @pl.when(rank == 0)
         def _():
-            pl.semaphore_wait(barrier, n_chan - 1)
+            pl.semaphore_wait(barrier, devices - 1)
             pl.semaphore_signal(go_sem, inc=1, device_id={"cyl": 1}, device_id_type=mesh_id)
 
         @pl.when(rank == 1)
@@ -282,132 +288,196 @@
             far_copy(d, n // pieces, n % pieces).start()
         return carry
 
-    lax.fori_loop(0, pieces, start_far, 0)
     for d in range(1, n_cyl):
         exp_copy(d).start()
+    lax.fori_loop(0, pieces, start_far, 0)
     lax.fori_loop(1, stages, start_own, 0)
     lax.fori_loop(pieces, stages * pieces, start_far, 0)
     fine_copy.wait()
+
     own_exps.wait()
-    ns_copy.wait()
     for d in range(1, n_cyl):
         exp_copy(d).wait()
     chans = exps_ref.shape[2]
-    lane = lax.broadcasted_iota(jnp.int32, (chans, own * UP), 1) // UP + rank * own
-    pick = (lane == lax.broadcasted_iota(jnp.int32, (chans, own * UP), 0)).astype(jnp.float32)
+    lane = lax.broadcasted_iota(jnp.int32, (chans, own * UP), 1)
+    chan = lax.broadcasted_iota(jnp.int32, (chans, own * UP), 0) - rank * own
     exps = jnp.concatenate([exps_ref[i] for i in range(n_cyl)], axis=0).astype(jnp.float32)
-    spread_exps = jnp.dot(exps, pick, preferred_element_type=jnp.float32)
-    scale = jnp.exp2(2.0 * spread_exps) / (pols * blocks)
+
+    def scale_of(pick):
+        spread = jnp.dot(exps, pick.astype(jnp.float32), preferred_element_type=jnp.float32)
+        return jnp.exp2(2.0 * spread) / (pols * blocks)
+
+    scale = scale_of(chan == lane // UP)
     for g in range(steps):
-        scale_ref[g] = scale[:, g * wide : (g + 1) * wide]
+        for o in range(n_cyl):
+            scale_ref[g, o] = scale[o * per : (o + 1) * per, g * wide : (g + 1) * wide]
+    lane, chan = lane[:, :wide], chan[:, :wide]
+    for h in range(per):
+        scale = scale_of(chan == h * part + lane % slim // UP)
+        for o in range(n_cyl):
+            row = scale[o * per : o * per + 1]
+            for e in range(1, per):
+                row = jnp.where(lane[:1] // slim == e, scale[o * per + e : o * per + e + 1], row)
+            head_scale_ref[h, o] = row
+
+    def fine_piece(s, i):
+        fine = fine_ref[...]
+        for d in range(1, n_cyl):
+            far_arrived(d, s, i).wait()
+        for c0 in range(piece):
+            ch = i * piece + c0
+            for p in range(pols):
+                for j in range(blocks):
+                    rows = jnp.concatenate(
+                        [
+                            held_ref[o, s, ch, c, p, j * UP : (j + 1) * UP, r * feeds : (r + 1) * feeds]
+                            for o in range(n_cyl)
+                            for c in range(per)
+                            for r in range(2)
+                        ],
+                        axis=0,
+                    )
+                    got = jnp.dot(fine, rows, preferred_element_type=jnp.float32)
+                    low, high = got[:, :half], got[:, half:]
+                    both = ((low + high).astype(jnp.bfloat16), (low - high).astype(jnp.bfloat16))
+                    for odd in range(2):
+                        for r in range(2):
+                            for e in range(cyls):
+                                at = (r * cyls + e) * UP
+                                mid_ref[p * blocks + j, odd, e, ch, :, r * half : (r + 1) * half] = (
+                                    both[odd][at : at + UP]
+                                )
+
+    def fine_pieces(s, first, last):
+        def one(i, carry):
+            fine_piece(s, i)
+            return carry
+
+        lax.fori_loop(first, last, one, 0)
+
+    def powers(owner, first, count):
+        parts = []
+        for odd in range(2):
+            total = None
+            for b in range(pols * blocks):
+                block = mid_ref[b, odd, pl.ds(owner * per, per), first : first + count]
+                spectra = lax.dot_general(
+                    ns_ref[odd], block.reshape(per * count * UP, feeds), (((1,), (1,)), ((), ())),
+                    preferred_element_type=jnp.float32,
+                )
+                squared = spectra * spectra
+                power = squared[:half] + squared[half:]
+                total = power if total is None else total + power
+            parts.append(total)
+        return parts
+
+    def by_chip(parts, factor):
+        scaled = [(part * factor).reshape(n_chan, near // 2, wide) for part in parts]
+        return jnp.concatenate(scaled, axis=1).astype(jnp.bfloat16)
+
+    def send_all(source_ref, target_ref, out_sem, in_sem):
+        def send(i, carry):
+            peer = lax.rem(me + 1 + i, devices)
+            to = peer // n_cyl
+            owner = lax.rem(peer, n_cyl)
+
+            @pl.when(peer == me)
+            def _():
+                pltpu.make_async_copy(source_ref.at[owner, to], target_ref.at[me], in_sem).start()
+
+            @pl.when(peer != me)
+            def _():
+                pltpu.make_async_remote_copy(
+                    src_ref=source_ref.at[owner, to],
+                    dst_ref=target_ref.at[me],
+                    send_sem=out_sem,
+                    recv_sem=in_sem,
+                    device_id={"chan": to, "cyl": owner},
+                    device_id_type=mesh_id,
+                ).start()
+
+            return carry
+
+        lax.fori_loop(0, devices, send, 0)
+
+    own_copy(0).wait()
+    for h in range(per):
+        fine_pieces(0, h * part // piece, (h + 1) * part // piece)
+        if h == 0:
+            ns_copy.wait()
+
+        def head_owner(owner, carry):
+            head_out_ref[h, owner] = by_chip(powers(owner, h * part, part), head_scale_ref[h, owner])
+            return carry
+
+        lax.fori_loop(0, n_cyl, head_owner, 0)
+        if h == 0:
+            all_here()
+        send_all(head_out_ref.at[h], head_in_ref.at[h], head_send_sem, head_recv_sem.at[h])
 
     def one_stage(s, carry):
         own_copy(s).wait()
-        fine = fine_ref[...]
-
-        def one_piece(i, inner):
-            for d in range(1, n_cyl):
-                far_arrived(d, s, i).wait()
-            for c0 in range(piece):
-                ch = i * piece + c0
-                for p in range(pols):
-                    for j in range(blocks):
-                        rows = jnp.concatenate(
-                            [
-                                held_ref[o, s, ch, c, p, j * UP : (j + 1) * UP, r * feeds : (r + 1) * feeds]
-                                for o in range(n_cyl)
-                                for c in range(per)
-                                for r in range(2)
-                            ],
-                            axis=0,
-                        )
-                        got = jnp.dot(fine, rows, preferred_element_type=jnp.float32)
-                        low, high = got[:, :half], got[:, half:]
-                        both = ((low + high).astype(jnp.bfloat16), (low - high).astype(jnp.bfloat16))
-                        for odd in range(2):
-                            for r in range(2):
-                                for e in range(cyls):
-                                    at = (r * cyls + e) * UP
-                                    mid_ref[p * blocks + j, odd, e, ch, :, r * half : (r + 1) * half] = (
-                                        both[odd][at : at + UP]
-                                    )
+        fine_pieces(s, 0, pieces)
+
+        def one_owner(owner, inner):
+            parts = powers(owner, 0, group)
+            for e in range(per):
+                send_ref[s - 1, owner, :, e] = by_chip(
+                    [part[:, e * wide : (e + 1) * wide] for part in parts],
+                    scale_ref[s // FRAMES, owner, e : e + 1, :],
+                )
             return inner
 
-        lax.fori_loop(0, pieces, one_piece, 0)
-        for owner in range(n_cyl):
-            parts = []
-            for odd in range(2):
-                ns = ns_ref[odd]
-                total = None
-                for b in range(pols * blocks):
-                    block = mid_ref[b, odd, owner * per : (owner + 1) * per].reshape(per * wide, feeds)
-                    spectra = lax.dot_general(
-                        ns, block, (((1,), (1,)), ((), ())), preferred_element_type=jnp.float32
-                    )
-                    squared = spectra * spectra
-                    power = squared[:half] + squared[half:]
-                    total = power if total is None else total + power
-                parts.append(total)
-            for e in range(per):
-                factor = scale_ref[s // FRAMES, owner * per + e : owner * per + e + 1, :]
-                scaled = [
-                    (part[:, e * wide : (e + 1) * wide] * factor).reshape(n_chan, near // 2, wide)
-                    for part in parts
-                ]
-                send_ref[s, owner, :, e] = jnp.concatenate(scaled, axis=1).astype(jnp.bfloat16)
-
-            if owner == 0:
-                pl.when(s == 0)(all_here)
-
-            def send(i, inner):
-                side = lax.rem(chip // (n_chan // 2) + 1 + i // (n_chan // 2), 2)
-                to = side * (n_chan // 2) + lax.rem(chip + 1 + i, n_chan // 2)
-                here = jnp.logical_and(to == chip, rank == owner)
-
-                @pl.when(here)
-                def _():
-                    pltpu.make_async_copy(
-                        send_ref.at[s, owner, to], recv_ref.at[s, me], recv_sem.at[s]
-                    ).start()
-
-                @pl.when(jnp.logical_not(here))
-                def _():
-                    pltpu.make_async_remote_copy(
-                        src_ref=send_ref.at[s, owner, to],
-                        dst_ref=recv_ref.at[s, me],
-                        send_sem=send_sem,
-                        recv_sem=recv_sem.at[s],
-                        device_id={"chan": to, "cyl": owner},
-                        device_id_type=pl.DeviceIdType.MESH,
-                    ).start()
-
-                return inner
-
-            lax.fori_loop(0, n_chan, send, 0)
-        return carry
-
-    lax.fori_loop(0, stages, one_stage, 0)
+        lax.fori_loop(0, n_cyl, one_owner, 0)
+        send_all(send_ref.at[s - 1], recv_ref.at[s - 1], send_sem, recv_sem.at[s - 1])
+        return carry
+
+    lax.fori_loop(1, stages, one_stage, 0)
 
     depth = devices * stages
 
+    several = math.gcd(4, devices)
+
+    def place(s, source, e, tile):
+        row = (source * steps + s // FRAMES) * FRAMES + s % FRAMES
+        for odd in range(2):
+            at = (e * near + odd) * depth + row
+            out_ref[pl.ds(at, near // 2, 2 * depth), :] = tile[odd * (near // 2) : (odd + 1) * (near // 2)]
+
+    for h in range(per):
+        pltpu.make_async_copy(head_in_ref.at[h], head_in_ref.at[h], head_recv_sem.at[h]).wait()
+    slot = lax.broadcasted_iota(jnp.int32, (near, wide), 1) // slim
+
+    def spread_head(source, carry):
+        tiles = [head_in_ref[h, source].astype(jnp.float32) for h in range(per)]
+        for e in range(per):
+            tile = tiles[e]
+            for h in range(per):
+                if h != e:
+                    moved = pltpu.roll(tiles[h], (h - e) * slim % wide, 1)
+                    tile = jnp.where(slot == h, moved, tile)
+            place(0, source, e, tile)
+        return carry
+
+    lax.fori_loop(0, devices, spread_head, 0)
+
     def spread_stage(s, carry):
-        pltpu.make_async_copy(recv_ref.at[s], recv_ref.at[s], recv_sem.at[s]).wait()
-
-        def one(source, inner):
-            row = (source * steps + s // FRAMES) * FRAMES + s % FRAMES
-            for e in range(per):
-                tile = recv_ref[s, source, e].astype(jnp.float32)
-                for odd in range(2):
-                    at = (e * near + odd) * depth + row
-                    out_ref[pl.ds(at, near // 2, 2 * depth), :] = tile[odd * (near // 2) : (odd + 1) * (near // 2)]
+        pltpu.make_async_copy(recv_ref.at[s - 1], recv_ref.at[s - 1], recv_sem.at[s - 1]).wait()
+
+        def some(n, inner):
+            for k in range(several):
+                for e in range(per):
+                    source = n * several + k
+                    place(s, source, e, recv_ref[s - 1, source, e].astype(jnp.float32))
             return inner
 
-        lax.fori_loop(0, devices, one, 0)
-        return carry
-
-    lax.fori_loop(0, stages, spread_stage, 0)
-    sent = recv_ref.at[:, : devices - 1]
-    pltpu.make_async_copy(sent, sent, send_sem).wait()
+        lax.fori_loop(0, devices // several, some, 0)
+        return carry
+
+    lax.fori_loop(1, stages, spread_stage, 0)
+    for ref, sem in ((head_in_ref, head_send_sem), (recv_ref, send_sem)):
+        sent = ref.at[:, : devices - 1]
+        pltpu.make_async_copy(sent, sent, sem).wait()
     for d in range(1, n_cyl):
         pltpu.make_async_copy(held_ref.at[0], held_ref.at[0], volt_send_sem.at[d]).wait()
 
@@ -438,10 +508,13 @@
         scratch_shapes=[
             pltpu.VMEM((n_cyl, stages, group, per, pols, span, inputs), jnp.bfloat16),
             pltpu.VMEM((pols * blocks, 2, cyls, group, UP, feeds), jnp.bfloat16),
-            pltpu.VMEM((stages, n_cyl, n_chan, per, near, wide), jnp.bfloat16),
-            pltpu.VMEM((stages, devices, per, near, wide), jnp.bfloat16),
+            pltpu.VMEM((per, n_cyl, n_chan, near, wide), jnp.bfloat16),
+            pltpu.VMEM((stages - 1, n_cyl, n_chan, per, near, wide), jnp.bfloat16),
+            pltpu.VMEM((per, devices, near, wide), jnp.bfloat16),
+            pltpu.VMEM((stages - 1, devices, per, near, wide), jnp.bfloat16),
             pltpu.VMEM((n_cyl, per, chans), jnp.int32),
-            pltpu.VMEM((steps, cyls, wide), jnp.float32),
+            pltpu.VMEM((per, n_cyl, 1, wide), jnp.float32),
+            pltpu.VMEM((steps, n_cyl, per, wide), jnp.float32),
             pltpu.VMEM(fine.shape, jnp.bfloat16),
             pltpu.VMEM(ns.shape, jnp.bfloat16),
             dma((stages,)),
@@ -452,7 +525,9 @@
             dma((n_cyl,)),
             dma((2,)),
             dma,
-            dma((stages,)),
+            dma((per,)),
+            dma,
+            dma((stages - 1,)),
             pltpu.SemaphoreType.REGULAR,
             pltpu.SemaphoreType.REGULAR,
         ],
@@ -471,7 +546,7 @@
     feeds = inputs // 2
     return (
         n_cyl == 2
-        and n_chan % 2 == 0
+        and per in (1, 2)
         and own % (128 // UP) == 0
         and feeds % (16 * n_chan) == 0
         and feeds % 256 == 0

time: 59.7 us -> 57 us (0.955); the launches traced: 58.9 us -> 56.8 us
  Pallas kernels: 56.8 us -> 54.8 us
    pallas_call x1, Pallas kernels: 56.8 us -> 54.8 us  [fused(): pl.pallas_call(functools.partial(fused_kernel, n_chan, n_cyl), out_shape=...]
where the time goes in v3:
time: 57 us; the launch traced here: 56.8 us
  Pallas kernels  54.8 us (96%)
  local copies, waits for them, and re-layouts  2.02 us (4%)
    pallas_call x1, Pallas kernels, fused(): pl.pallas_call(functools.partial(fused_kernel, n_chan, n_cyl), out_shape=...  54.8 us
    unnamed x1, local copies, waits for them, and re-layouts  2.02 us

profile of v3, /device:TPU:0, one launch (start us, length us, event | category | flops | bytes accessed | tf_op | source)
XLA Modules:
  0.0 56.8 jit_solution(18346510085653502059)
XLA Ops:
  0.0 54.8 %fused.1 = f32[8192,128]{1,0:T(8,128)S(1)} custom-call(bf16[64,2,2,64,512]{4,3,2,1,0:T(8,128)(2,1)} %volts_ref.1, s32[2,64]{1,0:T(2,128)} %bitcast.7, bf16[128,128]{1,0:T(8,128)(2,1)} %constant.4.clone.fine_hbm, bf16[2,256,256]{2,1,0:T(8,128)(2,1)} %constant.5.clone.ns_hbm), custom_call_target="tpu_custom_call" | custom-call | tf_op jit(solution)/shard_map/fused/pallas_call | solution.py:503
  54.8 2.0 %copy.7 = f32[2,16,2,16384]{3,2,1,0:T(2,128)} copy(f32[2,16,2,16384]{3,2,1,0:T(2,128)S(1)} %bitcast.6) | data formatting | bytes 8388608

commit v4 on v3

--- a/solution.py
+++ b/solution.py
@@ -197,8 +197,8 @@
     own = steps * group
     wide = group * UP
     near = feeds // n_chan
-    part = group // per
-    slim = part * UP
+    share = group // per
+    slim = share * UP
 
     def volt_rows(to, s, first, count):
         at = to * own + (s // FRAMES) * group + first
@@ -313,7 +313,7 @@
             scale_ref[g, o] = scale[o * per : (o + 1) * per, g * wide : (g + 1) * wide]
     lane, chan = lane[:, :wide], chan[:, :wide]
     for h in range(per):
-        scale = scale_of(chan == h * part + lane % slim // UP)
+        scale = scale_of(chan == h * share + lane % slim // UP)
         for o in range(n_cyl):
             row = scale[o * per : o * per + 1]
             for e in range(1, per):
@@ -355,14 +355,14 @@
 
         lax.fori_loop(first, last, one, 0)
 
-    def powers(owner, first, count):
+    def powers(beams, first, count):
         parts = []
         for odd in range(2):
             total = None
             for b in range(pols * blocks):
-                block = mid_ref[b, odd, pl.ds(owner * per, per), first : first + count]
+                block = mid_ref[b, odd, beams, first : first + count]
                 spectra = lax.dot_general(
-                    ns_ref[odd], block.reshape(per * count * UP, feeds), (((1,), (1,)), ((), ())),
+                    ns_ref[odd], block.reshape(-1, feeds), (((1,), (1,)), ((), ())),
                     preferred_element_type=jnp.float32,
                 )
                 squared = spectra * spectra
@@ -402,15 +402,15 @@
 
     own_copy(0).wait()
     for h in range(per):
-        fine_pieces(0, h * part // piece, (h + 1) * part // piece)
+        fine_pieces(0, h * share // piece, (h + 1) * share // piece)
         if h == 0:
             ns_copy.wait()
 
-        def head_owner(owner, carry):
-            head_out_ref[h, owner] = by_chip(powers(owner, h * part, part), head_scale_ref[h, owner])
-            return carry
-
-        lax.fori_loop(0, n_cyl, head_owner, 0)
+        parts = powers(pl.ds(0, cyls), h * share, share)
+        for o in range(n_cyl):
+            head_out_ref[h, o] = by_chip(
+                [part[:, o * wide : (o + 1) * wide] for part in parts], head_scale_ref[h, o]
+            )
         if h == 0:
             all_here()
         send_all(head_out_ref.at[h], head_in_ref.at[h], head_send_sem, head_recv_sem.at[h])
@@ -420,7 +420,7 @@
         fine_pieces(s, 0, pieces)
 
         def one_owner(owner, inner):
-            parts = powers(owner, 0, group)
+            parts = powers(pl.ds(owner * per, per), 0, group)
             for e in range(per):
                 send_ref[s - 1, owner, :, e] = by_chip(
                     [part[:, e * wide : (e + 1) * wide] for part in parts],

time: 57 us -> 56.5 us (level)
  no operation moved by 1% of the time
where the time goes in v4:
time: 56.5 us; the launch traced here: 56.4 us
  Pallas kernels  54.4 us (96%)
  local copies, waits for them, and re-layouts  2.02 us (4%)
    pallas_call x1, Pallas kernels, fused(): pl.pallas_call(functools.partial(fused_kernel, n_chan, n_cyl), out_shape=...  54.4 us
    unnamed x1, local copies, waits for them, and re-layouts  2.02 us

profile of v4, /device:TPU:0, one launch (start us, length us, event | category | flops | bytes accessed | tf_op | source)
XLA Modules:
  0.0 56.4 jit_solution(16319153396046495451)
XLA Ops:
  0.0 54.4 %fused.1 = f32[8192,128]{1,0:T(8,128)S(1)} custom-call(bf16[64,2,2,64,512]{4,3,2,1,0:T(8,128)(2,1)} %volts_ref.1, s32[2,64]{1,0:T(2,128)} %bitcast.7, bf16[128,128]{1,0:T(8,128)(2,1)} %constant.4.clone.fine_hbm, bf16[2,256,256]{2,1,0:T(8,128)(2,1)} %constant.5.clone.ns_hbm), custom_call_target="tpu_custom_call" | custom-call | tf_op jit(solution)/shard_map/fused/pallas_call | solution.py:503
  54.4 2.0 %copy.7 = f32[2,16,2,16384]{3,2,1,0:T(2,128)} copy(f32[2,16,2,16384]{3,2,1,0:T(2,128)S(1)} %bitcast.6) | data formatting | bytes 8388608

commit v5 on v4

--- a/solution.py
+++ b/solution.py
@@ -376,29 +376,21 @@
         return jnp.concatenate(scaled, axis=1).astype(jnp.bfloat16)
 
     def send_all(source_ref, target_ref, out_sem, in_sem):
-        def send(i, carry):
-            peer = lax.rem(me + 1 + i, devices)
-            to = peer // n_cyl
-            owner = lax.rem(peer, n_cyl)
-
-            @pl.when(peer == me)
-            def _():
-                pltpu.make_async_copy(source_ref.at[owner, to], target_ref.at[me], in_sem).start()
-
-            @pl.when(peer != me)
-            def _():
-                pltpu.make_async_remote_copy(
-                    src_ref=source_ref.at[owner, to],
-                    dst_ref=target_ref.at[me],
-                    send_sem=out_sem,
-                    recv_sem=in_sem,
-                    device_id={"chan": to, "cyl": owner},
-                    device_id_type=mesh_id,
-                ).start()
-
-            return carry
-
-        lax.fori_loop(0, devices, send, 0)
+        for i in range(1, devices):
+            turned = rank + i % n_cyl
+            over = turned >= n_cyl
+            owner = jnp.where(over, turned - n_cyl, turned)
+            ahead = chip + jnp.where(over, i // n_cyl + 1, i // n_cyl)
+            to = jnp.where(ahead >= n_chan, ahead - n_chan, ahead)
+            pltpu.make_async_remote_copy(
+                src_ref=source_ref.at[owner, to],
+                dst_ref=target_ref.at[me],
+                send_sem=out_sem,
+                recv_sem=in_sem,
+                device_id={"chan": to, "cyl": owner},
+                device_id_type=mesh_id,
+            ).start()
+        pltpu.make_async_copy(source_ref.at[rank, chip], target_ref.at[me], in_sem).start()
 
     own_copy(0).wait()
     for h in range(per):

time: 56.5 us -> 56.4 us (level)
  no operation moved by 1% of the time
where the time goes in v5:
time: 56.4 us; the launch traced here: 56.2 us
  Pallas kernels  54.2 us (96%)
  local copies, waits for them, and re-layouts  2.02 us (4%)
    pallas_call x1, Pallas kernels, fused(): pl.pallas_call(functools.partial(fused_kernel, n_chan, n_cyl), out_shape=...  54.2 us
    unnamed x1, local copies, waits for them, and re-layouts  2.02 us

profile of v5, /device:TPU:0, one launch (start us, length us, event | category | flops | bytes accessed | tf_op | source)
XLA Modules:
  0.0 56.2 jit_solution(361855076064145880)
XLA Ops:
  0.0 54.2 %fused.1 = f32[8192,128]{1,0:T(8,128)S(1)} custom-call(bf16[64,2,2,64,512]{4,3,2,1,0:T(8,128)(2,1)} %volts_ref.1, s32[2,64]{1,0:T(2,128)} %bitcast.7, bf16[128,128]{1,0:T(8,128)(2,1)} %constant.4.clone.fine_hbm, bf16[2,256,256]{2,1,0:T(8,128)(2,1)} %constant.5.clone.ns_hbm), custom_call_target="tpu_custom_call" | custom-call | tf_op jit(solution)/shard_map/fused/pallas_call | solution.py:495
  54.2 2.0 %copy.7 = f32[2,16,2,16384]{3,2,1,0:T(2,128)} copy(f32[2,16,2,16384]{3,2,1,0:T(2,128)S(1)} %bitcast.6) | data formatting | bytes 8388608

commit v6 on v5

--- a/solution.py
+++ b/solution.py
@@ -241,17 +241,19 @@
     barrier = pltpu.get_barrier_semaphore()
     mesh_id = pl.DeviceIdType.MESH
 
-    @pl.when(rank == 0)
-    def _():
-        pl.semaphore_signal(barrier, inc=1, device_id={"cyl": 1}, device_id_type=mesh_id)
-
-    @pl.when(rank == 1)
+    lead = n_cyl - 1
+
+    @pl.when(rank == lead)
     def _():
         pl.semaphore_signal(barrier, inc=1, device_id={"cyl": 0}, device_id_type=mesh_id)
 
+    @pl.when(rank != lead)
+    def _():
+        pl.semaphore_signal(barrier, inc=1, device_id={"cyl": lead}, device_id_type=mesh_id)
+
     def greet(i, carry):
         to = lax.rem(chip + i, n_chan)
-        pl.semaphore_signal(barrier, inc=1, device_id={"chan": to, "cyl": 0}, device_id_type=mesh_id)
+        pl.semaphore_signal(barrier, inc=1, device_id={"chan": to, "cyl": lead}, device_id_type=mesh_id)
         return carry
 
     lax.fori_loop(1, n_chan, greet, 0)
@@ -260,22 +262,22 @@
     own_exps.start()
     ns_copy.start()
 
-    @pl.when(rank == 1)
+    @pl.when(rank != lead)
     def _():
         pl.semaphore_wait(barrier, 1)
-        pl.semaphore_signal(pair_sem, inc=1, device_id={"cyl": 0}, device_id_type=mesh_id)
-
-    @pl.when(rank == 0)
+        pl.semaphore_signal(pair_sem, inc=1, device_id={"cyl": lead}, device_id_type=mesh_id)
+
+    @pl.when(rank == lead)
     def _():
         pl.semaphore_wait(pair_sem, 1)
 
     def all_here():
-        @pl.when(rank == 0)
+        @pl.when(rank == lead)
         def _():
             pl.semaphore_wait(barrier, devices - 1)
-            pl.semaphore_signal(go_sem, inc=1, device_id={"cyl": 1}, device_id_type=mesh_id)
-
-        @pl.when(rank == 1)
+            pl.semaphore_signal(go_sem, inc=1, device_id={"cyl": 0}, device_id_type=mesh_id)
+
+        @pl.when(rank != lead)
         def _():
             pl.semaphore_wait(go_sem, 1)
 

time: 56.4 us -> 56 us (level)
  no operation moved by 1% of the time
where the time goes in v6:
time: 56 us; the launch traced here: 55.9 us
  Pallas kernels  53.9 us (96%)
  local copies, waits for them, and re-layouts  2.02 us (4%)
    pallas_call x1, Pallas kernels, fused(): pl.pallas_call(functools.partial(fused_kernel, n_chan, n_cyl), out_shape=...  53.9 us
    unnamed x1, local copies, waits for them, and re-layouts  2.02 us

profile of v6, /device:TPU:0, one launch (start us, length us, event | category | flops | bytes accessed | tf_op | source)
XLA Modules:
  0.0 55.9 jit_solution(18144458526097676672)
XLA Ops:
  0.0 53.9 %fused.1 = f32[8192,128]{1,0:T(8,128)S(1)} custom-call(bf16[64,2,2,64,512]{4,3,2,1,0:T(8,128)(2,1)} %volts_ref.1, s32[2,64]{1,0:T(2,128)} %bitcast.7, bf16[128,128]{1,0:T(8,128)(2,1)} %constant.4.clone.fine_hbm, bf16[2,256,256]{2,1,0:T(8,128)(2,1)} %constant.5.clone.ns_hbm), custom_call_target="tpu_custom_call" | custom-call | tf_op jit(solution)/shard_map/fused/pallas_call | solution.py:497
  53.9 2.0 %copy.7 = f32[2,16,2,16384]{3,2,1,0:T(2,128)} copy(f32[2,16,2,16384]{3,2,1,0:T(2,128)S(1)} %bitcast.6) | data formatting | bytes 8388608

commit v7 on v6

--- a/solution.py
+++ b/solution.py
@@ -357,57 +357,79 @@
 
         lax.fori_loop(first, last, one, 0)
 
-    def powers(beams, first, count):
+    def powers(beams, first, count, rows=None):
         parts = []
         for odd in range(2):
             total = None
+            if rows is None:
+                ns = ns_ref[odd]
+            else:
+                ns = jnp.concatenate([ns_ref[odd, pl.ds(r * half + rows, half // 2)] for r in range(2)], axis=0)
+            kept = ns.shape[0] // 2
             for b in range(pols * blocks):
                 block = mid_ref[b, odd, beams, first : first + count]
                 spectra = lax.dot_general(
-                    ns_ref[odd], block.reshape(-1, feeds), (((1,), (1,)), ((), ())),
+                    ns, block.reshape(-1, feeds), (((1,), (1,)), ((), ())),
                     preferred_element_type=jnp.float32,
                 )
                 squared = spectra * spectra
-                power = squared[:half] + squared[half:]
+                power = squared[:kept] + squared[kept:]
                 total = power if total is None else total + power
             parts.append(total)
         return parts
 
     def by_chip(parts, factor):
-        scaled = [(part * factor).reshape(n_chan, near // 2, wide) for part in parts]
+        scaled = [(part * factor).reshape(-1, near // 2, wide) for part in parts]
         return jnp.concatenate(scaled, axis=1).astype(jnp.bfloat16)
 
-    def send_all(source_ref, target_ref, out_sem, in_sem):
-        for i in range(1, devices):
-            turned = rank + i % n_cyl
-            over = turned >= n_cyl
-            owner = jnp.where(over, turned - n_cyl, turned)
-            ahead = chip + jnp.where(over, i // n_cyl + 1, i // n_cyl)
-            to = jnp.where(ahead >= n_chan, ahead - n_chan, ahead)
-            pltpu.make_async_remote_copy(
-                src_ref=source_ref.at[owner, to],
-                dst_ref=target_ref.at[me],
-                send_sem=out_sem,
-                recv_sem=in_sem,
-                device_id={"chan": to, "cyl": owner},
-                device_id_type=mesh_id,
-            ).start()
+    def send_to(source_ref, target_ref, out_sem, in_sem, peer):
+        owner = lax.rem(peer, n_cyl)
+        to = lax.div(peer, n_cyl)
+        pltpu.make_async_remote_copy(
+            src_ref=source_ref.at[owner, to],
+            dst_ref=target_ref.at[me],
+            send_sem=out_sem,
+            recv_sem=in_sem,
+            device_id={"chan": to, "cyl": owner},
+            device_id_type=mesh_id,
+        ).start()
+
+    def send_ring(base, count, source_ref, target_ref, out_sem, in_sem):
+        at = me - base
+        for i in range(1, count):
+            peer = base + jnp.where(at + i >= count, at + i - count, at + i)
+            send_to(source_ref, target_ref, out_sem, in_sem, peer)
         pltpu.make_async_copy(source_ref.at[rank, chip], target_ref.at[me], in_sem).start()
+
+    side = lax.div(chip, n_chan // 2)
+    many = devices // 2
+
+    def send_other_side(*refs):
+        at = me - side * many
+        base = (1 - side) * many
+        for i in range(many):
+            send_to(*refs, base + jnp.where(at + i >= many, at + i - many, at + i))
 
     own_copy(0).wait()
     for h in range(per):
         fine_pieces(0, h * share // piece, (h + 1) * share // piece)
         if h == 0:
             ns_copy.wait()
-
-        parts = powers(pl.ds(0, cyls), h * share, share)
-        for o in range(n_cyl):
-            head_out_ref[h, o] = by_chip(
-                [part[:, o * wide : (o + 1) * wide] for part in parts], head_scale_ref[h, o]
-            )
-        if h == 0:
-            all_here()
-        send_all(head_out_ref.at[h], head_in_ref.at[h], head_send_sem, head_recv_sem.at[h])
+        refs = (head_out_ref.at[h], head_in_ref.at[h], head_send_sem, head_recv_sem.at[h])
+        for turn in range(2):
+            which = jnp.where(side == turn, 1, 0)
+            rows = pl.multiple_of(which * (half // 2), half // 2)
+            parts = powers(pl.ds(0, cyls), h * share, share, rows)
+            for o in range(n_cyl):
+                head_out_ref[h, o, pl.ds(which * (n_chan // 2), n_chan // 2)] = by_chip(
+                    [part[:, o * wide : (o + 1) * wide] for part in parts], head_scale_ref[h, o]
+                )
+            if turn == 0:
+                if h == 0:
+                    all_here()
+                send_other_side(*refs)
+            else:
+                send_ring(side * many, many, *refs)
 
     def one_stage(s, carry):
         own_copy(s).wait()
@@ -423,7 +445,7 @@
             return inner
 
         lax.fori_loop(0, n_cyl, one_owner, 0)
-        send_all(send_ref.at[s - 1], recv_ref.at[s - 1], send_sem, recv_sem.at[s - 1])
+        send_ring(0, devices, send_ref.at[s - 1], recv_ref.at[s - 1], send_sem, recv_sem.at[s - 1])
         return carry
 
     lax.fori_loop(1, stages, one_stage, 0)
@@ -540,6 +562,7 @@
     feeds = inputs // 2
     return (
         n_cyl == 2
+        and n_chan % 2 == 0
         and per in (1, 2)
         and own % (128 // UP) == 0
         and feeds % (16 * n_chan) == 0

time: 56 us -> 55.9 us (level)
  no operation moved by 1% of the time
where the time goes in v7:
time: 55.9 us; the launch traced here: 55.8 us
  Pallas kernels  53.8 us (96%)
  local copies, waits for them, and re-layouts  2.02 us (4%)
    pallas_call x1, Pallas kernels, fused(): pl.pallas_call(functools.partial(fused_kernel, n_chan, n_cyl), out_shape=...  53.8 us
    unnamed x1, local copies, waits for them, and re-layouts  2.02 us

profile of v7, /device:TPU:0, one launch (start us, length us, event | category | flops | bytes accessed | tf_op | source)
XLA Modules:
  0.0 55.8 jit_solution(16380241343914561673)
XLA Ops:
  0.0 53.8 %fused.1 = f32[8192,128]{1,0:T(8,128)S(1)} custom-call(bf16[64,2,2,64,512]{4,3,2,1,0:T(8,128)(2,1)} %volts_ref.1, s32[2,64]{1,0:T(2,128)} %bitcast.7, bf16[128,128]{1,0:T(8,128)(2,1)} %constant.4.clone.fine_hbm, bf16[2,256,256]{2,1,0:T(8,128)(2,1)} %constant.5.clone.ns_hbm), custom_call_target="tpu_custom_call" | custom-call | tf_op jit(solution)/shard_map/fused/pallas_call | solution.py:519
  53.8 2.0 %copy.7 = f32[2,16,2,16384]{3,2,1,0:T(2,128)} copy(f32[2,16,2,16384]{3,2,1,0:T(2,128)S(1)} %bitcast.6) | data formatting | bytes 8388608

commit v8 on v7

--- a/solution.py
+++ b/solution.py
@@ -256,7 +256,6 @@
         pl.semaphore_signal(barrier, inc=1, device_id={"chan": to, "cyl": lead}, device_id_type=mesh_id)
         return carry
 
-    lax.fori_loop(1, n_chan, greet, 0)
     own_copy(0).start()
     fine_copy.start()
     own_exps.start()
@@ -292,7 +291,9 @@
 
     for d in range(1, n_cyl):
         exp_copy(d).start()
-    lax.fori_loop(0, pieces, start_far, 0)
+    lax.fori_loop(0, pieces // 2, start_far, 0)
+    lax.fori_loop(1, n_chan, greet, 0)
+    lax.fori_loop(pieces // 2, pieces, start_far, 0)
     lax.fori_loop(1, stages, start_own, 0)
     lax.fori_loop(pieces, stages * pieces, start_far, 0)
     fine_copy.wait()
@@ -452,7 +453,7 @@
 
     depth = devices * stages
 
-    several = math.gcd(4, devices)
+    several = math.gcd(8, devices)
 
     def place(s, source, e, tile):
         row = (source * steps + s // FRAMES) * FRAMES + s % FRAMES

time: 55.9 us -> 55.8 us (level)
  no operation moved by 1% of the time
where the time goes in v8:
time: 55.8 us; the launch traced here: 55.7 us
  Pallas kernels  53.6 us (96%)
  local copies, waits for them, and re-layouts  2.02 us (4%)
    pallas_call x1, Pallas kernels, fused(): pl.pallas_call(functools.partial(fused_kernel, n_chan, n_cyl), out_shape=...  53.6 us
    unnamed x1, local copies, waits for them, and re-layouts  2.02 us

profile of v8, /device:TPU:0, one launch (start us, length us, event | category | flops | bytes accessed | tf_op | source)
XLA Modules:
  0.0 55.7 jit_solution(9321687935622840290)
XLA Ops:
  0.0 53.6 %fused.1 = f32[8192,128]{1,0:T(8,128)S(1)} custom-call(bf16[64,2,2,64,512]{4,3,2,1,0:T(8,128)(2,1)} %volts_ref.1, s32[2,64]{1,0:T(2,128)} %bitcast.7, bf16[128,128]{1,0:T(8,128)(2,1)} %constant.4.clone.fine_hbm, bf16[2,256,256]{2,1,0:T(8,128)(2,1)} %constant.5.clone.ns_hbm), custom_call_target="tpu_custom_call" | custom-call | tf_op jit(solution)/shard_map/fused/pallas_call | solution.py:520
  53.7 2.0 %copy.7 = f32[2,16,2,16384]{3,2,1,0:T(2,128)} copy(f32[2,16,2,16384]{3,2,1,0:T(2,128)S(1)} %bitcast.6) | data formatting | bytes 8388608

commit v9 on v7

--- a/solution.py
+++ b/solution.py
@@ -445,14 +445,14 @@
             return inner
 
         lax.fori_loop(0, n_cyl, one_owner, 0)
-        send_ring(0, devices, send_ref.at[s - 1], recv_ref.at[s - 1], send_sem, recv_sem.at[s - 1])
+        send_ring(0, devices, send_ref.at[s - 1], recv_ref.at[s - 1], send_sem, recv_sem.at[s - 1, side])
         return carry
 
     lax.fori_loop(1, stages, one_stage, 0)
 
     depth = devices * stages
 
-    several = math.gcd(4, devices)
+    several = math.gcd(4, many)
 
     def place(s, source, e, tile):
         row = (source * steps + s // FRAMES) * FRAMES + s % FRAMES
@@ -477,20 +477,23 @@
 
     lax.fori_loop(0, devices, spread_head, 0)
 
-    def spread_stage(s, carry):
-        pltpu.make_async_copy(recv_ref.at[s - 1], recv_ref.at[s - 1], recv_sem.at[s - 1]).wait()
+    def spread_side(turn, carry):
+        s = 1 + turn // 2
+        which = lax.rem(side + turn, 2)
+        arrived = recv_ref.at[s - 1, pl.ds(which * many, many)]
+        pltpu.make_async_copy(arrived, arrived, recv_sem.at[s - 1, which]).wait()
 
         def some(n, inner):
             for k in range(several):
                 for e in range(per):
-                    source = n * several + k
+                    source = which * many + n * several + k
                     place(s, source, e, recv_ref[s - 1, source, e].astype(jnp.float32))
             return inner
 
-        lax.fori_loop(0, devices // several, some, 0)
-        return carry
-
-    lax.fori_loop(1, stages, spread_stage, 0)
+        lax.fori_loop(0, many // several, some, 0)
+        return carry
+
+    lax.fori_loop(0, 2 * (stages - 1), spread_side, 0)
     for ref, sem in ((head_in_ref, head_send_sem), (recv_ref, send_sem)):
         sent = ref.at[:, : devices - 1]
         pltpu.make_async_copy(sent, sent, sem).wait()
@@ -543,7 +546,7 @@
             dma,
             dma((per,)),
             dma,
-            dma((stages - 1,)),
+            dma((stages - 1, 2)),
             pltpu.SemaphoreType.REGULAR,
             pltpu.SemaphoreType.REGULAR,
         ],

time: 55.9 us -> 55.8 us (level)
  no operation moved by 1% of the time
where the time goes in v9:
time: 55.8 us; the launch traced here: 55.6 us
  Pallas kernels  53.6 us (96%)
  local copies, waits for them, and re-layouts  2.02 us (4%)
    pallas_call x1, Pallas kernels, fused(): pl.pallas_call(functools.partial(fused_kernel, n_chan, n_cyl), out_shape=...  53.6 us
    unnamed x1, local copies, waits for them, and re-layouts  2.02 us

profile of v9, /device:TPU:0, one launch (start us, length us, event | category | flops | bytes accessed | tf_op | source)
XLA Modules:
  0.0 55.6 jit_solution(3818076676462184531)
XLA Ops:
  0.0 53.6 %fused.1 = f32[8192,128]{1,0:T(8,128)S(1)} custom-call(bf16[64,2,2,64,512]{4,3,2,1,0:T(8,128)(2,1)} %volts_ref.1, s32[2,64]{1,0:T(2,128)} %bitcast.7, bf16[128,128]{1,0:T(8,128)(2,1)} %constant.4.clone.fine_hbm, bf16[2,256,256]{2,1,0:T(8,128)(2,1)} %constant.5.clone.ns_hbm), custom_call_target="tpu_custom_call" | custom-call | tf_op jit(solution)/shard_map/fused/pallas_call | solution.py:522
  53.6 2.0 %copy.7 = f32[2,16,2,16384]{3,2,1,0:T(2,128)} copy(f32[2,16,2,16384]{3,2,1,0:T(2,128)S(1)} %bitcast.6) | data formatting | bytes 8388608
